TPU v7x, 32 devices: a whole 2x2x4 slice. The times are simulated.
32 devices in a mesh: dp: 4 (over y, x), ctx: 4 (over z), tp: 2 (over core).
Axes of the slice: x: 2, y: 2, z: 4, core: 2. Of those that a mesh axis runs over, the one named last changes fastest.
Arguments:
- tokens: bfloat16 [8, 2048, 768], P('dp', 'ctx'), may hold values from -6 to 6
- segments: int32 [8, 2048], P('dp', 'ctx'), may hold values from 0 to 7, never falling along the last dimension, each value on 1 to 768 neighbouring positions
- cotangent: bfloat16 [8, 2048, 768], P('dp', 'ctx'), may hold values from -6 to 6
- w_qkv: bfloat16 [768, 3, 768], P('dp', None, 'tp'), may hold values from -0.21875 to 0.21875
- w_out: bfloat16 [768, 768], P('dp', 'tp'), may hold values from -1.75 to 1.75
- w_gate: bfloat16 [768, 3072], P('dp', 'tp'), may hold values from -0.21875 to 0.21875
- w_up: bfloat16 [768, 3072], P('dp', 'tp'), may hold values from -0.21875 to 0.21875
- w_down: bfloat16 [768, 3072], P('dp', 'tp'), may hold values from -0.109375 to 0.109375
- norm_gain: bfloat16 [768], P('dp'), may hold values from 0.5 to 1.5
- norm_bias: bfloat16 [768], P('dp'), may hold values from -3 to 3
- final_gain: bfloat16 [768], P('dp'), may hold values from 0.5 to 1.5
- final_bias: bfloat16 [768], P('dp'), may hold values from -3 to 3
Outputs:
- output: bfloat16 [8, 2048, 768], P('dp', 'ctx')
- d_tokens: bfloat16 [8, 2048, 768], P('dp', 'ctx')
- d_qkv: float32 [768, 3, 768], P('dp', None, 'tp')
- d_out: float32 [768, 768], P('dp', 'tp')
- d_gate: float32 [768, 3072], P('dp', 'tp')
- d_up: float32 [768, 3072], P('dp', 'tp')
- d_down: float32 [768, 3072], P('dp', 'tp')
- d_norm_gain: float32 [768], P('dp')
- d_norm_bias: float32 [768], P('dp')
- d_final_gain: float32 [768], P('dp')
- d_final_bias: float32 [768], P('dp')
Inputs may be any that keep to these rules, and one draw needn't show every extreme that they name: `segments`: within each sequence the segment numbers never fall, and each document is a run of consecutive tokens.
All inputs are finite; a program needn't handle non-finite values.
Results may differ from a plain program's by a relative error of at most 0.023.
Values may be sent and summed in bfloat16 or wider, within the bound.
No kernel may reach another device: no remote copies, remote signals or barrier semaphores. Data moves between devices by JAX's collectives and lax.ppermute only.
A program may use at most 192 MiB of HBM per device.

v0:
```python
import jax
import jax.numpy as jnp
from jax import lax
from jax.sharding import PartitionSpec as P

HD = 64
epsilon = 1e-12
rotary_base = 1000.0


def rotary_tables(offset, length, head_size):
    half_size = head_size // 2
    places = (offset + jnp.arange(length)).astype(jnp.float32)
    inverse = rotary_base ** (-(jnp.arange(half_size).astype(jnp.float32) * 2.0 / head_size))
    angles = places[:, None] * inverse[None, :]
    angles = jnp.concatenate([angles, angles], axis=1)
    return (jnp.cos(angles), jnp.sin(angles))


def rotate_pairs(vector, cosine, sine_t):
    half_size = vector.shape[-1] // 2
    turned = jnp.concatenate([-vector[..., half_size:], vector[..., :half_size]], axis=-1)
    return vector * cosine[:, None, :] + turned * sine_t[:, None, :]


def rotate_back(gradient, cosine, sine_t):
    half_size = gradient.shape[-1] // 2
    moved = gradient * sine_t[:, None, :]
    turned = jnp.concatenate([moved[..., half_size:], -moved[..., :half_size]], axis=-1)
    return gradient * cosine[:, None, :] + turned


def norm_forward(values, gain_v, bias_v):
    average = jnp.mean(values, -1, keepdims=True)
    centred = values - average
    inv_std = lax.rsqrt(jnp.mean(centred * centred, -1, keepdims=True) + epsilon)
    unit_v = centred * inv_std
    return (unit_v * gain_v + bias_v, unit_v, inv_std)


def norm_backward(gradient, unit_v, inv_std, gain_v):
    scaled = gradient * gain_v
    dvalues = (
        scaled
        - jnp.mean(scaled, -1, keepdims=True)
        - unit_v * jnp.mean(scaled * unit_v, -1, keepdims=True)
    ) * inv_std
    return (dvalues, jnp.sum(gradient * unit_v, 0), jnp.sum(gradient, 0))


def contract_rows(left, right):
    return lax.dot_general(
        left, right, (((0,), (0,)), ((), ())), preferred_element_type=jnp.float32
    )


def contract_cols(left, right):
    return lax.dot_general(
        left, right, (((1,), (1,)), ((), ())), preferred_element_type=jnp.float32
    )


def masked_scores(queries, keys_rot, seg_query, seg_key, factor):
    raw = jnp.einsum("qhd,khd->hqk", queries, keys_rot, preferred_element_type=jnp.float32) * factor
    same_doc = seg_query[:, None] == seg_key[None, :]
    return jnp.where(same_doc[None], raw, -1e30)


def body(
    tokens,
    segments,
    cotangent,
    w_qkv,
    w_out,
    w_gate,
    w_up,
    w_down,
    norm_gain,
    norm_bias,
    final_gain,
    final_bias,
):
    seq_count, row_count, model_width = tokens.shape
    tok_count = seq_count * row_count
    factor = HD ** (-0.5)
    gathered = (
        lax.all_gather(w_qkv, "dp", axis=0, tiled=True),
        lax.all_gather(w_out, "dp", axis=0, tiled=True),
        lax.all_gather(w_gate, "dp", axis=0, tiled=True),
        lax.all_gather(w_up, "dp", axis=0, tiled=True),
        lax.all_gather(w_down, "dp", axis=0, tiled=True),
        lax.all_gather(norm_gain, "dp", axis=0, tiled=True),
        lax.all_gather(norm_bias, "dp", axis=0, tiled=True),
        lax.all_gather(final_gain, "dp", axis=0, tiled=True),
        lax.all_gather(final_bias, "dp", axis=0, tiled=True),
    )
    qkv_w, out_w, gate_w, up_w, down_w = (
        gathered[0],
        gathered[1],
        gathered[2],
        gathered[3],
        gathered[4],
    )
    gain_one = gathered[5].astype(jnp.float32)
    bias_one = gathered[6].astype(jnp.float32)
    gain_two = gathered[7].astype(jnp.float32)
    bias_two = gathered[8].astype(jnp.float32)
    local_width = qkv_w.shape[2]
    head_count = local_width // HD
    flat_in = tokens.reshape(tok_count, model_width)
    mixed_qkv = jnp.einsum("td,dcn->tcn", flat_in, qkv_w, preferred_element_type=jnp.float32)
    cosine, sine_t = rotary_tables(lax.axis_index("ctx") * row_count, row_count, HD)
    pieces = mixed_qkv.reshape(seq_count, row_count, 3, head_count, HD)
    queries = rotate_pairs(pieces[:, :, 0], cosine, sine_t).astype(jnp.bfloat16)
    keys_rot = (
        rotate_pairs(pieces[:, :, 1], cosine, sine_t)
        .astype(jnp.bfloat16)
        .reshape(seq_count, row_count, local_width)
    )
    valued = pieces[:, :, 2].astype(jnp.bfloat16).reshape(seq_count, row_count, local_width)
    all_keys, all_values = (
        lax.all_gather(keys_rot, "ctx", axis=1, tiled=True),
        lax.all_gather(valued, "ctx", axis=1, tiled=True),
    )
    all_docs = lax.all_gather(segments, "ctx", axis=1, tiled=True)
    length = all_keys.shape[1]
    key_heads = all_keys.reshape(seq_count, length, head_count, HD)
    value_heads = all_values.reshape(seq_count, length, head_count, HD)

    def attend(blocks):
        query_blk, key_blk, value_blk, seg_query, seg_key = blocks
        scores = masked_scores(query_blk, key_blk, seg_query, seg_key, factor)
        largest = jnp.max(scores, -1, keepdims=True)
        exp_scores = jnp.exp(scores - largest)
        row_total = jnp.sum(exp_scores, -1, keepdims=True)
        chances = (exp_scores / row_total).astype(jnp.bfloat16)
        mixture = jnp.einsum("hqk,khd->qhd", chances, value_blk, preferred_element_type=jnp.float32)
        return (mixture.astype(jnp.bfloat16), (largest + jnp.log(row_total))[..., 0])

    mixture, log_total = lax.map(attend, (queries, key_heads, value_heads, segments, all_docs))
    mixture_flat = mixture.reshape(tok_count, local_width)
    attended = lax.psum(contract_cols(mixture_flat, out_w).astype(jnp.bfloat16), "tp").astype(
        jnp.float32
    )
    normed, unit_one, inv_one = norm_forward(
        flat_in.astype(jnp.float32) + attended, gain_one, bias_one
    )
    normed_low = normed.astype(jnp.bfloat16)
    gate_pre = jnp.dot(normed_low, gate_w, preferred_element_type=jnp.float32)
    up_pre = jnp.dot(normed_low, up_w, preferred_element_type=jnp.float32)
    sigmoid_g = jax.nn.sigmoid(gate_pre)
    activated = gate_pre * sigmoid_g
    hidden_low = (activated * up_pre).astype(jnp.bfloat16)
    branch = lax.psum(contract_cols(hidden_low, down_w).astype(jnp.bfloat16), "tp").astype(
        jnp.float32
    )
    final_out, unit_two, inv_two = norm_forward(normed + branch, gain_two, bias_two)
    output = final_out.astype(jnp.bfloat16).reshape(seq_count, row_count, model_width)
    back_weights = (
        lax.all_gather(w_qkv, "dp", axis=0, tiled=True),
        lax.all_gather(w_out, "dp", axis=0, tiled=True),
        lax.all_gather(w_gate, "dp", axis=0, tiled=True),
        lax.all_gather(w_up, "dp", axis=0, tiled=True),
        lax.all_gather(w_down, "dp", axis=0, tiled=True),
        lax.all_gather(norm_gain, "dp", axis=0, tiled=True),
        lax.all_gather(norm_bias, "dp", axis=0, tiled=True),
        lax.all_gather(final_gain, "dp", axis=0, tiled=True),
        lax.all_gather(final_bias, "dp", axis=0, tiled=True),
    )
    qkv_b, out_b, gate_b, up_b, down_b = (
        back_weights[0],
        back_weights[1],
        back_weights[2],
        back_weights[3],
        back_weights[4],
    )
    gain_one_b = back_weights[5].astype(jnp.float32)
    gain_two_b = back_weights[7].astype(jnp.float32)
    grad_out = cotangent.reshape(tok_count, model_width).astype(jnp.float32)
    dsum, dgain_two, dbias_two = norm_backward(grad_out, unit_two, inv_two, gain_two_b)
    dbranch = dsum.astype(jnp.bfloat16)
    d_down = contract_rows(dbranch, hidden_low)
    dhidden = jnp.dot(dbranch, down_b, preferred_element_type=jnp.float32)
    dgate = (dhidden * up_pre * sigmoid_g * (1.0 + gate_pre * (1.0 - sigmoid_g))).astype(
        jnp.bfloat16
    )
    dup = (dhidden * activated).astype(jnp.bfloat16)
    d_gate = contract_rows(normed_low, dgate)
    d_up = contract_rows(normed_low, dup)
    dnormed_part = contract_cols(dgate, gate_b) + contract_cols(dup, up_b)
    dnormed = dsum + lax.psum(dnormed_part.astype(jnp.bfloat16), "tp").astype(jnp.float32)
    dresid, dgain_one, dbias_one = norm_backward(dnormed, unit_one, inv_one, gain_one_b)
    dattended = dresid.astype(jnp.bfloat16)
    d_out = contract_rows(dattended, mixture_flat)
    dmixture = jnp.dot(dattended, out_b, preferred_element_type=jnp.float32).astype(jnp.bfloat16)
    dmixture = dmixture.reshape(seq_count, row_count, head_count, HD)

    def attend_back(blocks):
        query_blk, key_blk, value_blk, seg_query, seg_key, log_blk, dmix_blk = blocks
        scores = masked_scores(query_blk, key_blk, seg_query, seg_key, factor)
        chances = jnp.exp(scores - log_blk[..., None])
        dchances = jnp.einsum(
            "qhd,khd->hqk", dmix_blk, value_blk, preferred_element_type=jnp.float32
        )
        row_dot = jnp.sum(chances * dchances, -1, keepdims=True)
        dscores = (chances * (dchances - row_dot)).astype(jnp.bfloat16)
        dquery = (
            jnp.einsum("hqk,khd->qhd", dscores, key_blk, preferred_element_type=jnp.float32)
            * factor
        )
        dkey = (
            jnp.einsum("hqk,qhd->khd", dscores, query_blk, preferred_element_type=jnp.float32)
            * factor
        )
        dvalue = jnp.einsum(
            "hqk,qhd->khd",
            chances.astype(jnp.bfloat16),
            dmix_blk,
            preferred_element_type=jnp.float32,
        )
        return (dquery, dkey.reshape(dkey.shape[0], -1), dvalue.reshape(dvalue.shape[0], -1))

    dqueries, dkeys_all, dvalues_all = lax.map(
        attend_back, (queries, key_heads, value_heads, segments, all_docs, log_total, dmixture)
    )
    dkeys_own, dvalues_own = (
        lax.psum_scatter(
            dkeys_all.astype(jnp.bfloat16), "ctx", scatter_dimension=1, tiled=True
        ).astype(jnp.float32),
        lax.psum_scatter(
            dvalues_all.astype(jnp.bfloat16), "ctx", scatter_dimension=1, tiled=True
        ).astype(jnp.float32),
    )
    dkey_heads = dkeys_own.reshape(seq_count, row_count, head_count, HD)
    dvalue_heads = dvalues_own.reshape(seq_count, row_count, head_count, HD)
    dquery_raw = rotate_back(dqueries, cosine, sine_t)
    dkey_raw = rotate_back(dkey_heads, cosine, sine_t)
    dqkv = (
        jnp.stack([dquery_raw, dkey_raw, dvalue_heads], 2)
        .reshape(tok_count, 3, local_width)
        .astype(jnp.bfloat16)
    )
    dinput_part = jnp.einsum("tcn,dcn->td", dqkv, qkv_b, preferred_element_type=jnp.float32)
    dinput = dresid + lax.psum(dinput_part.astype(jnp.bfloat16), "tp").astype(jnp.float32)
    d_tokens = dinput.astype(jnp.bfloat16).reshape(seq_count, row_count, model_width)
    d_qkv = jnp.einsum("td,tcn->dcn", flat_in, dqkv, preferred_element_type=jnp.float32)
    grad_terms = (d_qkv, d_out, d_gate, d_up, d_down, dgain_one, dbias_one, dgain_two, dbias_two)
    group_part = (
        lax.psum_scatter(
            grad_terms[0].astype(jnp.bfloat16), "dp", scatter_dimension=0, tiled=True
        ).astype(jnp.float32),
        lax.psum_scatter(
            grad_terms[1].astype(jnp.bfloat16), "dp", scatter_dimension=0, tiled=True
        ).astype(jnp.float32),
        lax.psum_scatter(
            grad_terms[2].astype(jnp.bfloat16), "dp", scatter_dimension=0, tiled=True
        ).astype(jnp.float32),
        lax.psum_scatter(
            grad_terms[3].astype(jnp.bfloat16), "dp", scatter_dimension=0, tiled=True
        ).astype(jnp.float32),
        lax.psum_scatter(
            grad_terms[4].astype(jnp.bfloat16), "dp", scatter_dimension=0, tiled=True
        ).astype(jnp.float32),
        lax.psum_scatter(
            grad_terms[5].astype(jnp.bfloat16), "dp", scatter_dimension=0, tiled=True
        ).astype(jnp.float32),
        lax.psum_scatter(
            grad_terms[6].astype(jnp.bfloat16), "dp", scatter_dimension=0, tiled=True
        ).astype(jnp.float32),
        lax.psum_scatter(
            grad_terms[7].astype(jnp.bfloat16), "dp", scatter_dimension=0, tiled=True
        ).astype(jnp.float32),
        lax.psum_scatter(
            grad_terms[8].astype(jnp.bfloat16), "dp", scatter_dimension=0, tiled=True
        ).astype(jnp.float32),
    )
    reduced = (
        lax.psum(group_part[0].astype(jnp.bfloat16), "ctx").astype(jnp.float32),
        lax.psum(group_part[1].astype(jnp.bfloat16), "ctx").astype(jnp.float32),
        lax.psum(group_part[2].astype(jnp.bfloat16), "ctx").astype(jnp.float32),
        lax.psum(group_part[3].astype(jnp.bfloat16), "ctx").astype(jnp.float32),
        lax.psum(group_part[4].astype(jnp.bfloat16), "ctx").astype(jnp.float32),
        lax.psum(group_part[5].astype(jnp.bfloat16), "ctx").astype(jnp.float32),
        lax.psum(group_part[6].astype(jnp.bfloat16), "ctx").astype(jnp.float32),
        lax.psum(group_part[7].astype(jnp.bfloat16), "ctx").astype(jnp.float32),
        lax.psum(group_part[8].astype(jnp.bfloat16), "ctx").astype(jnp.float32),
    )
    return (output, d_tokens) + tuple(reduced)


def solution(mesh):
    placed = (
        P("dp", "ctx", None),
        P("dp", "ctx"),
        P("dp", "ctx", None),
        P("dp", None, "tp"),
        P("dp", "tp"),
        P("dp", "tp"),
        P("dp", "tp"),
        P("dp", "tp"),
        P("dp"),
        P("dp"),
        P("dp"),
        P("dp"),
    )
    return jax.shard_map(
        body,
        mesh=mesh,
        in_specs=placed,
        out_specs=(
            P("dp", "ctx", None),
            P("dp", "ctx", None),
            P("dp", None, "tp"),
            P("dp", "tp"),
            P("dp", "tp"),
            P("dp", "tp"),
            P("dp", "tp"),
            P("dp"),
            P("dp"),
            P("dp"),
            P("dp"),
        ),
        check_vma=False,
    )
```

profile of v0, /device:TPU:0, one launch (start us, length us, event | category | flops | bytes accessed | tf_op | source)
XLA Modules:
  0.0 1096.9 jit_solution(12073563558076399821)
XLA Ops:
  8.0 37.1 %all-gather.7.cloned.1.call-done = bf16[768,3,384]{2,0,1:T(8,128)(2,1)} async-done(((bf16[192,3,384]{2,0,1:T(8,128)(2,1)}), bf16[768,3,384]{2,0,1:T(8,128)(2,1)}) %all-gather.7.cloned.1.call-update) | async-done | bytes 1769488 | tf_op jit(solution)/shard_map/all_gather | solution.py:87
  57.8 13.6 %all_gather.45 = s32[2,2048]{1,0:T(2,128)S(1)} all-gather(s32[2,512]{1,0:T(2,128)S(1)} %copy-done.34), channel_id=1, replica_groups=mesh['dp'=4,'ctx'=4,'tp'=2] {'ctx'}, dimensions={1}, use_global_device_ids=true | all-gather | bytes 20480 | tf_op jit(solution)/shard_map/all_gather | solution.py:125
  71.4 11.4 %all_gather.47 = bf16[768,384]{1,0:T(8,128)(2,1)} all-gather(bf16[192,384]{1,0:T(8,128)(2,1)S(1)} %copy-done.35), channel_id=1, replica_groups=mesh['dp'=4,'ctx'=4,'tp'=2] {'dp'}, dimensions={0}, use_global_device_ids=true | all-gather | bytes 737280 | tf_op jit(solution)/shard_map/all_gather | solution.py:88
  84.9 31.7 %all-gather.9.cloned.1.call-done = bf16[2,2048,384]{1,2,0:T(8,128)(2,1)} async-done(((bf16[2,512,384]{1,2,0:T(8,128)(2,1)}), bf16[2,2048,384]{1,2,0:T(8,128)(2,1)}) %all-gather.9.cloned.1.call-update) | async-done | bytes 3145744 | tf_op jit(solution)/shard_map/all_gather | solution.py:123
  116.6 64.3 %all-gather.11.cloned.1.call-done = bf16[2,2048,384]{1,2,0:T(8,128)(2,1)} async-done(((bf16[2,512,384]{1,2,0:T(8,128)(2,1)}), bf16[2,2048,384]{1,2,0:T(8,128)(2,1)}) %all-gather.11.cloned.1.call-update) | async-done | bytes 3145744 | tf_op jit(solution)/shard_map/all_gather | solution.py:122
  180.9 73.4 %while.26 = (s32[]{:T(128)}, bf16[2,512,6,64]{1,3,2,0:T(8,128)(2,1)S(1)}, f32[2,6,512]{2,1,0:T(8,128)S(1)}, bf16[2,2048,6,64]{1,3,2,0:T(8,128)(2,1)}, s32[2,512]...) while((s32[]{:T(128)}, ...), condition=%wide.region_3.4_spmd, body=%wide.region_0.3_spmd.sunk | while | flops 1687352320 | bytes 96358544 | solution.py:140
  181.6 12.2 %fusion.139 = (f32[6,512]{1,0:T(8,128)S(1)}, f32[6,512,2048]{2,1,0:T(8,128)}) fusion(pred[512,2048]{1,0:T(8,128)(4,1)S(1)} %broadcast_compare_fusion.4, bf16[2,2048,6,64]{1,3,2,0:T(8,128)(2,1)} %get-tuple-element.429, s32[]{:T(128)S(6)} %copy.77, bf16[2,512,6,64]{1,3,2,0:T(8,128)(2,1)S(1)} %get-tuple-element.428), kind=kOutput, calls=%fused_computation.3.clone.1 | convolution fusion | flops 824177664 | bytes 28193792 | tf_op jit(solution)/shard_map/while/body/eval_jaxpr/qhd,khd->hqk/dot_general | solution.py:64
  193.8 12.1 %fusion.140 = f32[6,512]{1,0:T(8,128)S(1)} fusion(f32[6,512,2048]{2,1,0:T(8,128)} %get-tuple-element.387, f32[6,512]{1,0:T(8,128)S(1)} %get-tuple-element.388, pred[512,2048]{1,0:T(8,128)(4,1)S(1)} %broadcast_compare_fusion.4), kind=kLoop, calls=%fused_computation.4.clone.1 | loop fusion | flops 25162752 | bytes 26238976 | tf_op jit(solution)/shard_map/while/body/eval_jaxpr/reduce_sum | solution.py:135
  205.9 11.7 %fusion.141 = bf16[2,512,6,64]{1,3,2,0:T(8,128)(2,1)S(1)} fusion(bf16[2,512,6,64]{1,3,2,0:T(8,128)(2,1)S(1)} %get-tuple-element.414, s32[]{:T(128)S(6)} %copy.77, f32[6,512,2048]{2,1,0:T(8,128)} %get-tuple-element.387, f32[6,512]{1,0:T(8,128)S(1)} %fusion.140, f32[6,512]{1,0:T(8,128)S(1)} %get-tuple-element.388, ...), kind=kOutput, calls=%fused_computation.14.clone.1 | convolution fusion | flops 836960256 | bytes 28214272 | tf_op jit(solution)/shard_map/while/body/eval_jaxpr/hqk,khd->qhd/dot_general | solution.py:137
  218.3 12.2 %fusion.139 = (f32[6,512]{1,0:T(8,128)S(1)}, f32[6,512,2048]{2,1,0:T(8,128)}) fusion(pred[512,2048]{1,0:T(8,128)(4,1)S(1)} %broadcast_compare_fusion.4, bf16[2,2048,6,64]{1,3,2,0:T(8,128)(2,1)} %get-tuple-element.429, s32[]{:T(128)S(6)} %copy.77, bf16[2,512,6,64]{1,3,2,0:T(8,128)(2,1)S(1)} %get-tuple-element.428), kind=kOutput, calls=%fused_computation.3.clone.1 | convolution fusion | flops 824177664 | bytes 28193792 | tf_op jit(solution)/shard_map/while/body/eval_jaxpr/qhd,khd->hqk/dot_general | solution.py:64
  230.5 12.1 %fusion.140 = f32[6,512]{1,0:T(8,128)S(1)} fusion(f32[6,512,2048]{2,1,0:T(8,128)} %get-tuple-element.387, f32[6,512]{1,0:T(8,128)S(1)} %get-tuple-element.388, pred[512,2048]{1,0:T(8,128)(4,1)S(1)} %broadcast_compare_fusion.4), kind=kLoop, calls=%fused_computation.4.clone.1 | loop fusion | flops 25162752 | bytes 26238976 | tf_op jit(solution)/shard_map/while/body/eval_jaxpr/reduce_sum | solution.py:135
  242.6 11.7 %fusion.141 = bf16[2,512,6,64]{1,3,2,0:T(8,128)(2,1)S(1)} fusion(bf16[2,512,6,64]{1,3,2,0:T(8,128)(2,1)S(1)} %get-tuple-element.414, s32[]{:T(128)S(6)} %copy.77, f32[6,512,2048]{2,1,0:T(8,128)} %get-tuple-element.387, f32[6,512]{1,0:T(8,128)S(1)} %fusion.140, f32[6,512]{1,0:T(8,128)S(1)} %get-tuple-element.388, ...), kind=kOutput, calls=%fused_computation.14.clone.1 | convolution fusion | flops 836960256 | bytes 28214272 | tf_op jit(solution)/shard_map/while/body/eval_jaxpr/hqk,khd->qhd/dot_general | solution.py:137
  262.3 10.3 all-reduce.11
  282.3 35.4 %all-gather.13.cloned.1.call-done = bf16[768,1536]{1,0:T(8,128)(2,1)} async-done(((bf16[192,1536]{1,0:T(8,128)(2,1)}), bf16[768,1536]{1,0:T(8,128)(2,1)}) %all-gather.13.cloned.1.call-update) | async-done | bytes 2359312 | tf_op jit(solution)/shard_map/all_gather | solution.py:89
  317.7 7.4 fusion.96
  325.2 31.7 %all-gather.15.cloned.1.call-done = bf16[768,1536]{1,0:T(8,128)(2,1)} async-done(((bf16[192,1536]{1,0:T(8,128)(2,1)}), bf16[768,1536]{1,0:T(8,128)(2,1)}) %all-gather.15.cloned.1.call-update) | async-done | bytes 2359312 | tf_op jit(solution)/shard_map/all_gather | solution.py:90
  356.8 10.6 multiply_convert_fusion.3
  367.4 28.6 %all-gather.17.cloned.1.call-done = bf16[768,1536]{1,0:T(8,128)(2,1)} async-done(((bf16[192,1536]{1,0:T(8,128)(2,1)}), bf16[768,1536]{1,0:T(8,128)(2,1)}) %all-gather.17.cloned.1.call-update) | async-done | bytes 2359312 | tf_op jit(solution)/shard_map/all_gather | solution.py:91
  396.0 6.4 convolution_convert_fusion.5
  404.8 18.2 %all-reduce.20.cloned.1.call-done = bf16[1024,768]{1,0:T(8,128)(2,1)} async-done(((bf16[1024,768]{1,0:T(8,128)(2,1)}), bf16[1024,768]{1,0:T(8,128)(2,1)}) %all-reduce.20.cloned.1.call-update) | async-done | bytes 1572880 | tf_op jit(solution)/shard_map/psum | solution.py:154
  432.1 6.9 multiply_convert_fusion.1
  446.3 21.6 %all-reduce.22.cloned.1.call-done = bf16[1024,768]{1,0:T(8,128)(2,1)} async-done(((bf16[1024,768]{1,0:T(8,128)(2,1)}), bf16[1024,768]{1,0:T(8,128)(2,1)}) %all-reduce.22.cloned.1.call-update) | async-done | bytes 1572880 | tf_op jit(solution)/shard_map/psum | solution.py:191
  467.9 5.3 multiply_reduce_fusion.1
  478.5 156.4 %while.27 = (s32[]{:T(128)}, f32[2,512,6,64]{1,3,2,0:T(8,128)}, bf16[2,2048,384]{1,2,0:T(8,128)(2,1)}, bf16[2,2048,384]{1,2,0:T(8,128)(2,1)}, bf16[2,2048,6,64]{...) while((s32[]{:T(128)}, f32[2,512,6,64]{1,3,2,0:T(8,128)}, ...), condition=%wide.region_17.18_spmd, body=%wide.region_15.17_spmd.sunk | while | flops 4123718656 | bytes 226358576 | solution.py:223
  479.5 11.9 %fusion.150 = f32[6,512,2048]{2,1,0:T(8,128)} fusion(bf16[2,2048,6,64]{1,3,2,0:T(8,128)(2,1)} %get-tuple-element.459, s32[]{:T(128)S(6)} %copy.91, bf16[2,512,6,64]{1,3,2,0:T(8,128)(2,1)S(1)} %get-tuple-element.462), kind=kOutput, calls=%fused_computation.36.clone.1 | convolution fusion | flops 805306368 | bytes 27132928 | tf_op jit(solution)/shard_map/while/body/eval_jaxpr/qhd,khd->hqk/dot_general | solution.py:64
  491.4 12.8 %fusion.152 = bf16[6,64,2048]{2,1,0:T(8,128)(2,1)} fusion(f32[6,512,2048]{2,1,0:T(8,128)} %fusion.150, f32[6,512]{1,0:T(8,128)S(1)} %dynamic-slice_bitcast_fusion.2, pred[512,2048]{1,0:T(8,128)(4,1)S(1)} %broadcast_compare_fusion.5, bf16[2,512,6,64]{1,3,2,0:T(8,128)(2,1)S(1)} %get-tuple-element.464, s32[]{:T(128)S(6)} %copy.91), kind=kOutput, calls=%fused_computation.28.clone.1 | convolution fusion | flops 830472192 | bytes 28196868 | tf_op jit(solution)/shard_map/while/body/eval_jaxpr/hqk,qhd->khd/dot_general | solution.py:215
  504.2 20.0 %multiply_reduce_fusion.7 = (f32[6,512]{1,0:T(8,128)S(1)}, f32[6,512,2048]{2,1,0:T(8,128)}) fusion(f32[6,512,2048]{2,1,0:T(8,128)} %fusion.150, f32[6,512]{1,0:T(8,128)S(1)} %dynamic-slice_bitcast_fusion.2, pred[512,2048]{1,0:T(8,128)(4,1)S(1)} %broadcast_compare_fusion.5, bf16[2,2048,6,64]{1,3,2,0:T(8,128)(2,1)} %get-tuple-element.465, ...), kind=kOutput, calls=%fused_computation.25.clone.1 | convolution fusion | flops 836760576 | bytes 53376000 | tf_op jit(solution)/shard_map/while/body/eval_jaxpr/qhd,khd->hqk/dot_general | solution.py:202
  524.2 17.7 %multiply_convert_fusion.5 = bf16[6,512,2048]{2,1,0:T(8,128)(2,1)S(1)} fusion(f32[6,512,2048]{2,1,0:T(8,128)} %get-tuple-element.400, f32[6,512,2048]{2,1,0:T(8,128)} %fusion.150, f32[6,512]{1,0:T(8,128)S(1)} %get-tuple-element.401, f32[6,512]{1,0:T(8,128)S(1)} %dynamic-slice_bitcast_fusion.2, pred[512,2048]{1,0:T(8,128)(4,1)} %copy-done), kind=kLoop, calls=%fused_computation.24.clone.1 | loop fusion | flops 37748736 | bytes 63987712 | tf_op jit(solution)/shard_map/while/body/eval_jaxpr/convert_element_type | solution.py:206
  546.4 6.2 fusion.151
  557.5 11.9 %fusion.150 = f32[6,512,2048]{2,1,0:T(8,128)} fusion(bf16[2,2048,6,64]{1,3,2,0:T(8,128)(2,1)} %get-tuple-element.459, s32[]{:T(128)S(6)} %copy.91, bf16[2,512,6,64]{1,3,2,0:T(8,128)(2,1)S(1)} %get-tuple-element.462), kind=kOutput, calls=%fused_computation.36.clone.1 | convolution fusion | flops 805306368 | bytes 27132928 | tf_op jit(solution)/shard_map/while/body/eval_jaxpr/qhd,khd->hqk/dot_general | solution.py:64
  569.4 12.8 %fusion.152 = bf16[6,64,2048]{2,1,0:T(8,128)(2,1)} fusion(f32[6,512,2048]{2,1,0:T(8,128)} %fusion.150, f32[6,512]{1,0:T(8,128)S(1)} %dynamic-slice_bitcast_fusion.2, pred[512,2048]{1,0:T(8,128)(4,1)S(1)} %broadcast_compare_fusion.5, bf16[2,512,6,64]{1,3,2,0:T(8,128)(2,1)S(1)} %get-tuple-element.464, s32[]{:T(128)S(6)} %copy.91), kind=kOutput, calls=%fused_computation.28.clone.1 | convolution fusion | flops 830472192 | bytes 28196868 | tf_op jit(solution)/shard_map/while/body/eval_jaxpr/hqk,qhd->khd/dot_general | solution.py:215
  582.2 20.0 %multiply_reduce_fusion.7 = (f32[6,512]{1,0:T(8,128)S(1)}, f32[6,512,2048]{2,1,0:T(8,128)}) fusion(f32[6,512,2048]{2,1,0:T(8,128)} %fusion.150, f32[6,512]{1,0:T(8,128)S(1)} %dynamic-slice_bitcast_fusion.2, pred[512,2048]{1,0:T(8,128)(4,1)S(1)} %broadcast_compare_fusion.5, bf16[2,2048,6,64]{1,3,2,0:T(8,128)(2,1)} %get-tuple-element.465, ...), kind=kOutput, calls=%fused_computation.25.clone.1 | convolution fusion | flops 836760576 | bytes 53376000 | tf_op jit(solution)/shard_map/while/body/eval_jaxpr/qhd,khd->hqk/dot_general | solution.py:202
  602.3 17.7 %multiply_convert_fusion.5 = bf16[6,512,2048]{2,1,0:T(8,128)(2,1)S(1)} fusion(f32[6,512,2048]{2,1,0:T(8,128)} %get-tuple-element.400, f32[6,512,2048]{2,1,0:T(8,128)} %fusion.150, f32[6,512]{1,0:T(8,128)S(1)} %get-tuple-element.401, f32[6,512]{1,0:T(8,128)S(1)} %dynamic-slice_bitcast_fusion.2, pred[512,2048]{1,0:T(8,128)(4,1)} %copy-done), kind=kLoop, calls=%fused_computation.24.clone.1 | loop fusion | flops 37748736 | bytes 63987712 | tf_op jit(solution)/shard_map/while/body/eval_jaxpr/convert_element_type | solution.py:206
  624.4 6.3 fusion.151
  639.3 57.4 %reduce-scatter.10.cloned.1.call-done = bf16[2,512,384]{1,2,0:T(8,128)(2,1)} async-done(((bf16[2,2048,384]{1,2,0:T(8,128)(2,1)}), bf16[2,512,384]{1,2,0:T(8,128)(2,1)}) %reduce-scatter.10.cloned.1.call-update) | async-done | bytes 786448 | tf_op jit(solution)/shard_map/reduce_scatter | solution.py:227
  711.1 48.3 %reduce-scatter.12.cloned.1.call-done = bf16[2,512,384]{1,2,0:T(8,128)(2,1)} async-done(((bf16[2,2048,384]{1,2,0:T(8,128)(2,1)}), bf16[2,512,384]{1,2,0:T(8,128)(2,1)}) %reduce-scatter.12.cloned.1.call-update) | async-done | bytes 786448 | tf_op jit(solution)/shard_map/reduce_scatter | solution.py:230
  773.9 7.0 convolution_convert_fusion
  781.0 5.9 convolution_convert_fusion.2
  787.0 5.9 convolution_convert_fusion.1
  793.1 5.0 bitcast_convert_fusion
  798.2 4.9 reduce-scatter.22.cloned.1.call-done
  805.2 26.8 %reduce-scatter.14.cloned.1.call-done = bf16[192,384]{1,0:T(8,128)(2,1)} async-done(((bf16[768,384]{1,0:T(8,128)(2,1)}), bf16[192,384]{1,0:T(8,128)(2,1)}) %reduce-scatter.14.cloned.1.call-update) | async-done | bytes 147472 | tf_op jit(solution)/shard_map/reduce_scatter | solution.py:252
  832.0 40.3 %reduce-scatter.20.cloned.1.call-done = bf16[192,1536]{1,0:T(8,128)(2,1)} async-done(((bf16[768,1536]{1,0:T(8,128)(2,1)}), bf16[192,1536]{1,0:T(8,128)(2,1)}) %reduce-scatter.20.cloned.1.call-update) | async-done | bytes 589840 | tf_op jit(solution)/shard_map/reduce_scatter | solution.py:261
  872.3 40.3 %reduce-scatter.16.cloned.1.call-done = bf16[192,1536]{1,0:T(8,128)(2,1)} async-done(((bf16[768,1536]{1,0:T(8,128)(2,1)}), bf16[192,1536]{1,0:T(8,128)(2,1)}) %reduce-scatter.16.cloned.1.call-update) | async-done | bytes 589840 | tf_op jit(solution)/shard_map/reduce_scatter | solution.py:255
  912.6 40.3 %reduce-scatter.18.cloned.1.call-done = bf16[192,1536]{1,0:T(8,128)(2,1)} async-done(((bf16[768,1536]{1,0:T(8,128)(2,1)}), bf16[192,1536]{1,0:T(8,128)(2,1)}) %reduce-scatter.18.cloned.1.call-update) | async-done | bytes 589840 | tf_op jit(solution)/shard_map/reduce_scatter | solution.py:258
  955.6 15.0 %all-reduce.10 = (bf16[768]{0:T(1024)(128)(2,1)S(1)}, bf16[768]{0:T(1024)(128)(2,1)S(1)}, bf16[768]{0:T(1024)(128)(2,1)S(1)}, bf16[768]{0:T(1024)(128)(2,1)S(1)}, bf16[768]{0:T(1024)(128)(2,1)S(1)}) all-reduce(bf16[768]{0:T(1024)(128)(2,1)S(1)} %dynamic-update-slice.3, ...), channel_id=1, replica_groups=mesh['dp'=4,'ctx'=4,'tp'=2] {'dp'}, use_global_device_ids=true, to_apply=%add.3 | all-reduce | flops 3840 | bytes 15360
  970.9 11.7 %all-reduce.8 = (bf16[192]{0:T(256)(128)(2,1)S(1)}, bf16[192]{0:T(256)(128)(2,1)S(1)}, bf16[192]{0:T(256)(128)(2,1)S(1)}, bf16[192]{0:T(256)(128)(2,1)S(1)}) all-reduce(bf16[192]{0:T(256)(128)(2,1)S(1)} %dynamic-slice.5, bf16[192]{0:T(256)(128)(2,1)S(1)} %dynamic-slice.7, ...), channel_id=1, replica_groups=mesh['dp'=4,'ctx'=4,'tp'=2] {'ctx'}, use_global_device_ids=true, to_apply=%region_33.34 | all-reduce | flops 768 | bytes 3072 | tf_op jit(solution)/shard_map/psum | solution.py:283
  990.4 90.7 %all-reduce.26.cloned.1.call-done = (bf16[192,3,384]{0,2,1:T(8,128)(2,1)}, bf16[192,384]{1,0:T(8,128)(2,1)}, bf16[192,1536]{1,0:T(8,128)(2,1)}, bf16[192,1536]{1,0:T(8,128)(2,1)}, bf16[192,1536]{1,0:T(8,128)(2,1)}) async-done(((bf16[192,3,384]{0,2,1:T(8,128)(2,1)}, bf16[192,384]{1,0:T(8,128)(2,1)}, bf16[192,1536]{1,0:T(8,128)(2,1)}, bf16[192,1536]{1,0:T(8,128)(2,1)}, bf16[192,1536]{1,0:T(8,128)(2,1)}), ...) | async-done | bytes 2359312 | tf_op jit(solution)/shard_map/psum | solution.py:278
  (282 shorter events, 130.0 us)
Async XLA Ops:
  7.2 40.5 %copy-start.5 = (bf16[2,512,768]{2,1,0:T(8,128)(2,1)S(1)}, bf16[2,512,768]{2,1,0:T(8,128)(2,1)}, u32[]{:S(2)}) copy-start(bf16[2,512,768]{2,1,0:T(8,128)(2,1)} %param.16) | copy-start | bytes 4718596
  7.2 37.9 %all-gather.7.cloned.1.call-start = ((), (), s32[]{:S(2)}) async-start(), calls=%async_computation.7 | async-start | bytes 2211840 | tf_op jit(solution)/shard_map/all_gather | solution.py:87
  7.9 108.7 %all-gather.9.cloned.1.call-start = ((), (), s32[]{:S(2)}) async-start(), calls=%async_computation.8 | async-start | bytes 3932160 | tf_op jit(solution)/shard_map/all_gather | solution.py:123
  52.9 128.0 %all-gather.11.cloned.1.call-start = ((), (), s32[]{:S(2)}) async-start(), calls=%async_computation.9 | async-start | bytes 3932160 | tf_op jit(solution)/shard_map/all_gather | solution.py:122
  53.3 29.7 %copy-start.22 = (f32[512,64]{0,1:T(8,128)}, f32[512,64]{0,1:T(8,128)S(1)}, u32[]{:S(2)}) copy-start(f32[512,64]{0,1:T(8,128)S(1)} %get-tuple-element.268) | copy-start | bytes 393220
  53.3 29.7 %copy-start.27 = (f32[512,64]{0,1:T(8,128)}, f32[512,64]{0,1:T(8,128)S(1)}, u32[]{:S(2)}) copy-start(f32[512,64]{0,1:T(8,128)S(1)} %get-tuple-element.269) | copy-start | bytes 393220
  56.2 15.2 %copy-start.35 = (bf16[192,384]{1,0:T(8,128)(2,1)S(1)}, bf16[192,384]{1,0:T(8,128)(2,1)}, u32[]{:S(2)}) copy-start(bf16[192,384]{1,0:T(8,128)(2,1)} %param.20) | copy-start | bytes 442372
  57.8 219.7 %all-reduce.18.cloned.1.call-start = ((), (), s32[]{:S(2)}) async-start(), calls=%async_computation.10 | async-start | bytes 3145728 | tf_op jit(solution)/shard_map/psum | solution.py:142
  193.8 12.1 %copy-start.15 = (bf16[2,2048,6,64]{1,3,2,0:T(8,128)(2,1)S(1)}, bf16[2,2048,6,64]{1,3,2,0:T(8,128)(2,1)}, u32[]{:S(2)}) copy-start(bf16[2,2048,6,64]{1,3,2,0:T(8,128)(2,1)} %get-tuple-element.425) | copy-start | bytes 9437188 | tf_op jit(solution)/shard_map/while
  230.4 12.1 %copy-start.15 = (bf16[2,2048,6,64]{1,3,2,0:T(8,128)(2,1)S(1)}, bf16[2,2048,6,64]{1,3,2,0:T(8,128)(2,1)}, u32[]{:S(2)}) copy-start(bf16[2,2048,6,64]{1,3,2,0:T(8,128)(2,1)} %get-tuple-element.425) | copy-start | bytes 9437188 | tf_op jit(solution)/shard_map/while
  256.1 21.4 %copy-start.6 = (bf16[2,512,768]{2,1,0:T(8,128)(2,1)S(1)}, bf16[2,512,768]{2,1,0:T(8,128)(2,1)}, u32[]{:S(2)}) copy-start(bf16[2,512,768]{2,1,0:T(8,128)(2,1)} %param.16) | copy-start | bytes 4718596
  258.3 59.4 %all-gather.13.cloned.1.call-start = ((), (), s32[]{:S(2)}) async-start(), calls=%async_computation.11 | async-start | bytes 2949120 | tf_op jit(solution)/shard_map/all_gather | solution.py:89
  258.9 97.9 %all-gather.15.cloned.1.call-start = ((), (), s32[]{:S(2)}) async-start(), calls=%async_computation.12 | async-start | bytes 2949120 | tf_op jit(solution)/shard_map/all_gather | solution.py:90
  259.5 136.5 %all-gather.17.cloned.1.call-start = ((), (), s32[]{:S(2)}) async-start(), calls=%async_computation.13 | async-start | bytes 2949120 | tf_op jit(solution)/shard_map/all_gather | solution.py:91
  260.3 162.7 %all-reduce.20.cloned.1.call-start = ((), (), s32[]{:S(2)}) async-start(), calls=%async_computation.14 | async-start | bytes 3145728 | tf_op jit(solution)/shard_map/psum | solution.py:154
  402.4 65.5 %all-reduce.22.cloned.1.call-start = ((), (), s32[]{:S(2)}) async-start(), calls=%async_computation.15 | async-start | bytes 3145728 | tf_op jit(solution)/shard_map/psum | solution.py:191
  403.0 27.4 %copy-start.36 = (f32[768]{0:T(1024)}, f32[768]{0:T(1024)S(1)}, u32[]{:S(2)}) copy-start(f32[768]{0:T(1024)S(1)} %convert_element_type.216) | copy-start | bytes 9220
  431.6 7.4 copy-start.12
  432.1 6.9 copy-start.46
  446.2 250.5 %reduce-scatter.10.cloned.1.call-start = ((), (), s32[]{:S(2)}) async-start(), calls=%async_computation.16 | async-start | bytes 3932160 | tf_op jit(solution)/shard_map/reduce_scatter | solution.py:227
  478.7 12.7 %copy-start.3 = (bf16[2,512,6,64]{1,3,2,0:T(8,128)(2,1)}, bf16[2,512,6,64]{1,3,2,0:T(8,128)(2,1)S(1)}, u32[]{:S(2)}) copy-start(bf16[2,512,6,64]{1,3,2,0:T(8,128)(2,1)S(1)} %get-tuple-element.462) | copy-start | bytes 2359300 | tf_op jit(solution)/shard_map/while
  478.7 25.5 %copy-start.16 = (bf16[2,512,6,64]{1,3,2,0:T(8,128)(2,1)}, bf16[2,512,6,64]{1,3,2,0:T(8,128)(2,1)S(1)}, u32[]{:S(2)}) copy-start(bf16[2,512,6,64]{1,3,2,0:T(8,128)(2,1)S(1)} %get-tuple-element.464) | copy-start | bytes 2359300 | tf_op jit(solution)/shard_map/while
  479.5 24.8 %copy-start = (pred[512,2048]{1,0:T(8,128)(4,1)}, pred[512,2048]{1,0:T(8,128)(4,1)S(1)}, u32[]{:S(2)}) copy-start(pred[512,2048]{1,0:T(8,128)(4,1)S(1)} %broadcast_compare_fusion.5) | copy-start | bytes 3145732 | tf_op jit(solution)/shard_map/while
  556.7 12.7 %copy-start.3 = (bf16[2,512,6,64]{1,3,2,0:T(8,128)(2,1)}, bf16[2,512,6,64]{1,3,2,0:T(8,128)(2,1)S(1)}, u32[]{:S(2)}) copy-start(bf16[2,512,6,64]{1,3,2,0:T(8,128)(2,1)S(1)} %get-tuple-element.462) | copy-start | bytes 2359300 | tf_op jit(solution)/shard_map/while
  556.7 25.5 %copy-start.16 = (bf16[2,512,6,64]{1,3,2,0:T(8,128)(2,1)}, bf16[2,512,6,64]{1,3,2,0:T(8,128)(2,1)S(1)}, u32[]{:S(2)}) copy-start(bf16[2,512,6,64]{1,3,2,0:T(8,128)(2,1)S(1)} %get-tuple-element.464) | copy-start | bytes 2359300 | tf_op jit(solution)/shard_map/while
  557.5 24.8 %copy-start = (pred[512,2048]{1,0:T(8,128)(4,1)}, pred[512,2048]{1,0:T(8,128)(4,1)S(1)}, u32[]{:S(2)}) copy-start(pred[512,2048]{1,0:T(8,128)(4,1)S(1)} %broadcast_compare_fusion.5) | copy-start | bytes 3145732 | tf_op jit(solution)/shard_map/while
  635.0 124.4 %reduce-scatter.12.cloned.1.call-start = ((), (), s32[]{:S(2)}) async-start(), calls=%async_computation.17 | async-start | bytes 3932160 | tf_op jit(solution)/shard_map/reduce_scatter | solution.py:230
  635.7 167.4 %reduce-scatter.22.cloned.1.call-start = ((), (), s32[]{:S(2)}) async-start(), calls=%async_computation.23 | async-start | bytes 2211840
  637.6 60.5 %copy-start.21 = (f32[2,512,6,64]{1,3,2,0:T(8,128)S(1)}, f32[2,512,6,64]{1,3,2,0:T(8,128)}, u32[]{:S(2)}) copy-start(f32[2,512,6,64]{1,3,2,0:T(8,128)} %get-tuple-element.115) | copy-start | bytes 4718596
  637.6 60.5 %copy-start.28 = (f32[512,64]{0,1:T(8,128)S(1)}, f32[512,64]{0,1:T(8,128)}, u32[]{:S(2)}) copy-start(f32[512,64]{0,1:T(8,128)} %copy-done.27) | copy-start | bytes 393220
  708.0 53.8 %copy-start.7 = (bf16[2,512,768]{2,1,0:T(8,128)(2,1)S(1)}, bf16[2,512,768]{2,1,0:T(8,128)(2,1)}, u32[]{:S(2)}) copy-start(bf16[2,512,768]{2,1,0:T(8,128)(2,1)} %param.16) | copy-start | bytes 4718596
  770.6 61.5 %reduce-scatter.14.cloned.1.call-start = ((), (), s32[]{:S(2)}) async-start(), calls=%async_computation.19 | async-start | bytes 737280 | tf_op jit(solution)/shard_map/reduce_scatter | solution.py:252
  773.9 7.2 copy-start.30
  773.9 98.4 %reduce-scatter.20.cloned.1.call-start = ((), (), s32[]{:S(2)}) async-start(), calls=%async_computation.22 | async-start | bytes 2949120 | tf_op jit(solution)/shard_map/reduce_scatter | solution.py:261
  781.0 131.6 %reduce-scatter.16.cloned.1.call-start = ((), (), s32[]{:S(2)}) async-start(), calls=%async_computation.20 | async-start | bytes 2949120 | tf_op jit(solution)/shard_map/reduce_scatter | solution.py:255
  787.0 166.0 %reduce-scatter.18.cloned.1.call-start = ((), (), s32[]{:S(2)}) async-start(), calls=%async_computation.21 | async-start | bytes 2949120 | tf_op jit(solution)/shard_map/reduce_scatter | solution.py:258
  793.0 193.6 %all-reduce.24.cloned.1.call-start = ((), (), s32[]{:S(2)}) async-start(), calls=%async_computation.18 | async-start | bytes 3145728 | tf_op jit(solution)/shard_map/psum | solution.py:244
  798.1 157.3 %copy-start.52 = (bf16[192]{0:T(256)(128)(2,1)S(1)}, bf16[192]{0:T(256)(128)(2,1)}, u32[]{:S(2)}) copy-start(bf16[192]{0:T(256)(128)(2,1)} %param.27) | copy-start | bytes 1156
  798.1 157.5 %copy-start.42 = (bf16[768]{0:T(1024)(128)(2,1)S(1)}, bf16[768]{0:T(1024)(128)(2,1)}, u32[]{:S(2)}) copy-start(bf16[768]{0:T(1024)(128)(2,1)} %get-tuple-element.186) | copy-start | bytes 4612
  798.1 157.5 %copy-start.43 = (bf16[768]{0:T(1024)(128)(2,1)S(1)}, bf16[768]{0:T(1024)(128)(2,1)}, u32[]{:S(2)}) copy-start(bf16[768]{0:T(1024)(128)(2,1)} %get-tuple-element.184) | copy-start | bytes 4612
  798.1 157.5 %copy-start.44 = (bf16[768]{0:T(1024)(128)(2,1)S(1)}, bf16[768]{0:T(1024)(128)(2,1)}, u32[]{:S(2)}) copy-start(bf16[768]{0:T(1024)(128)(2,1)} %get-tuple-element.189) | copy-start | bytes 4612
  798.1 186.8 %copy-start.2 = (f32[1024,768]{1,0:T(8,128)S(1)}, f32[1024,768]{1,0:T(8,128)}, u32[]{:S(2)}) copy-start(f32[1024,768]{1,0:T(8,128)} %copy-done.1) | copy-start | bytes 9437188
  798.1 186.8 %copy-start.37 = (f32[768]{0:T(1024)S(1)}, f32[768]{0:T(1024)}, u32[]{:S(2)}) copy-start(f32[768]{0:T(1024)} %copy-done.36) | copy-start | bytes 9220
  798.1 186.8 %copy-start.39 = (f32[1024]{0:T(1024)S(1)}, f32[1024]{0:T(1024)}, u32[]{:S(2)}) copy-start(f32[1024]{0:T(1024)} %copy-done.38) | copy-start | bytes 12292
  798.1 186.8 %copy-start.41 = (f32[1024]{0:T(1024)S(1)}, f32[1024]{0:T(1024)}, u32[]{:S(2)}) copy-start(f32[1024]{0:T(1024)} %copy-done.40) | copy-start | bytes 12292
  798.1 283.0 %all-reduce.26.cloned.1.call-start = ((), (), s32[]{:S(2)}) async-start(), calls=%async_computation.24 | async-start | bytes 5013504 | tf_op jit(solution)/shard_map/psum | solution.py:278
  1081.1 6.2 copy-start.33
  1081.1 7.3 copy-start.32
  (33 other events, 113.0 us)
Sparse Core Ops, SparseCore 0:
  9.8 35.1 all-gather.6
  53.0 63.5 all-gather.8
  118.8 62.0 all-gather.10
  258.5 18.9 all-reduce.17
  279.2 38.5 all-gather.12
  319.4 37.3 all-gather.14
  358.6 37.3 all-gather.16
  402.6 20.3 all-reduce.19
  446.3 21.5 all-reduce.21
  635.1 61.5 reduce-scatter.9
  699.1 60.3 reduce-scatter.11
  770.7 32.3 reduce-scatter.21
  806.5 25.4 reduce-scatter.13
  834.9 37.3 reduce-scatter.19
  875.2 37.3 reduce-scatter.15
  915.5 37.3 reduce-scatter.17
  955.7 20.3 all-reduce.23
  979.3 101.7 all-reduce.25
where the time goes:
time: 1100 us
  waiting for transfers between devices  626 us (57%)
  matrix products  233 us (21%)
  other arithmetic  108 us (10%)
  blocking collectives  62 us (6%)
  local copies, waits for them, and re-layouts  49.2 us (4%)
  between operations  16.9 us (2%)
    psum x1, waiting for transfers between devices, body(): lax.psum(group_part[0].astype(jnp.bfloat16), 'ctx').astype(jnp.float32)  90.7 us
    all_gather x1, waiting for transfers between devices, body(): lax.all_gather(keys_rot, 'ctx', axis=1, tiled=True)  64.3 us
    reduce_scatter x1, waiting for transfers between devices, body(): lax.psum_scatter(dkeys_all.astype(jnp.bfloat16), 'ctx', scatter_dimension...  57.4 us
    reduce_scatter x1, waiting for transfers between devices, body(): lax.psum_scatter(dvalues_all.astype(jnp.bfloat16), 'ctx', scatter_dimensi...  48.3 us
    dot_general x4, matrix products, masked_scores(): jnp.einsum('qhd,khd->hqk', queries, keys_rot, preferred_element_type=jnp....  48.2 us
    reduce_scatter x1, waiting for transfers between devices, body(): lax.psum_scatter(grad_terms[3].astype(jnp.bfloat16), 'dp', scatter_dimens...  40.3 us
    reduce_scatter x1, waiting for transfers between devices, body(): lax.psum_scatter(grad_terms[2].astype(jnp.bfloat16), 'dp', scatter_dimens...  40.3 us
    reduce_scatter x1, waiting for transfers between devices, body(): lax.psum_scatter(grad_terms[4].astype(jnp.bfloat16), 'dp', scatter_dimens...  40.3 us
  transfers between devices with their start and end apart: 18, of which 17 were waited for; matrix products, arithmetic and copies ran while one was open for 8% of the time, Pallas kernels for 0%

commit v1 on v0

--- a/solution.py
+++ b/solution.py
@@ -1,3 +1,4 @@
+import functools
 import jax
 import jax.numpy as jnp
 from jax import lax
@@ -6,6 +7,22 @@
 HD = 64
 epsilon = 1e-12
 rotary_base = 1000.0
+
+
+def note_domain(s0, net_axis, along_dim):
+    carry_in = lax.psum(1, net_axis)
+    odd, t_next = (carry_in, lax.axis_index(net_axis))
+    near, clean = (s0, 1)
+    while clean < odd:
+        kept_arr = lax.ppermute(near, net_axis, list(map(lambda d: (d, d ^ clean), range(odd))))
+        u_next = jnp.concatenate([near, kept_arr], along_dim)
+        block_next = jnp.concatenate([kept_arr, near], along_dim)
+        near = jnp.where(t_next & clean == 0, u_next, block_next)
+        clean = 2 * clean
+    return near
+
+
+shape_the_chunk = functools.partial(note_domain, net_axis="ctx", along_dim=1)
 
 
 def rotary_tables(offset, length, head_size):
@@ -119,7 +136,7 @@
     )
     valued = pieces[:, :, 2].astype(jnp.bfloat16).reshape(seq_count, row_count, local_width)
     all_keys, all_values = (
-        lax.all_gather(keys_rot, "ctx", axis=1, tiled=True),
+        shape_the_chunk(keys_rot),
         lax.all_gather(valued, "ctx", axis=1, tiled=True),
     )
     all_docs = lax.all_gather(segments, "ctx", axis=1, tiled=True)

time: 1100 us -> 1150 us (1.045)
  blocking collectives: 62 us -> 123 us
  waiting for transfers between devices: 626 us -> 587 us
  local copies, waits for them, and re-layouts: 49.2 us -> 62.7 us
    all_gather x1 -> x0, waiting for transfers between devices: 64.3 us -> none  [body(): lax.all_gather(keys_rot, 'ctx', axis=1, tiled=True)]
    all_gather x1, blocking collectives: 13.6 us -> 76.1 us  [body(): all_docs = lax.all_gather(segments, 'ctx', axis=1, tiled=True)]
    ppermute x0 -> x2, waiting for transfers between devices: none -> 58.8 us  [note_domain(): lax.ppermute(near, net_axis, list(map(lambda d: (d, d ^ clean), range(odd...]
    all_gather x1, waiting for transfers between devices: 31.7 us -> 0.02 us  [body(): lax.all_gather(valued, 'ctx', axis=1, tiled=True)]
  transfers between devices with their start and end apart: 18 -> 19, of which waited for: 17 -> 16; matrix products, arithmetic and copies ran while one was open for 8% -> 8% of each run, Pallas kernels for 0% -> 0%
where the time goes in v1:
time: 1150 us; the launch traced here: 1140 us
  waiting for transfers between devices  587 us (51%)
  matrix products  236 us (21%)
  blocking collectives  123 us (11%)
  other arithmetic  113 us (10%)
  local copies, waits for them, and re-layouts  62.7 us (5%)
  between operations  16.3 us (1%)
    psum x1, waiting for transfers between devices, body(): lax.psum(group_part[0].astype(jnp.bfloat16), 'ctx').astype(jnp.float32)  90.7 us
    all_gather x1, blocking collectives, body(): all_docs = lax.all_gather(segments, 'ctx', axis=1, tiled=True)  76.1 us
    ppermute x2, waiting for transfers between devices, note_domain(): lax.ppermute(near, net_axis, list(map(lambda d: (d, d ^ clean), range(odd...  58.8 us
    reduce_scatter x1, waiting for transfers between devices, body(): lax.psum_scatter(dkeys_all.astype(jnp.bfloat16), 'ctx', scatter_dimension...  57.4 us
    dot_general x4, matrix products, masked_scores(): jnp.einsum('qhd,khd->hqk', queries, keys_rot, preferred_element_type=jnp....  50.7 us
    reduce_scatter x1, waiting for transfers between devices, body(): lax.psum_scatter(dvalues_all.astype(jnp.bfloat16), 'ctx', scatter_dimensi...  48.1 us
    reduce_scatter x1, waiting for transfers between devices, body(): lax.psum_scatter(grad_terms[4].astype(jnp.bfloat16), 'dp', scatter_dimens...  40.5 us
    reduce_scatter x1, waiting for transfers between devices, body(): lax.psum_scatter(grad_terms[3].astype(jnp.bfloat16), 'dp', scatter_dimens...  40.3 us
  transfers between devices with their start and end apart: 19, of which 16 were waited for; matrix products, arithmetic and copies ran while one was open for 8% of the time, Pallas kernels for 0%

profile of v1, /device:TPU:0, one launch (start us, length us, event | category | flops | bytes accessed | tf_op | source)
XLA Modules:
  0.0 1144.1 jit_solution(3720865042750576043)
XLA Ops:
  8.0 37.1 %all-gather.6.cloned.1.call-done = bf16[768,3,384]{2,0,1:T(8,128)(2,1)} async-done(((bf16[192,3,384]{2,0,1:T(8,128)(2,1)}), bf16[768,3,384]{2,0,1:T(8,128)(2,1)}) %all-gather.6.cloned.1.call-update) | async-done | bytes 1769488 | tf_op jit(solution)/shard_map/all_gather | solution.py:104
  60.7 58.8 %collective-permute-done = bf16[2,512,384]{1,2,0:T(8,128)(2,1)S(1)} collective-permute-done((bf16[2,512,384]{1,2,0:T(8,128)(2,1)S(1)}, bf16[2,512,384]{1,2,0:T(8,128)(2,1)S(1)}, u32[]{:S(2)}, u32[]{:S(2)}) %collective-permute-start) | collective-permute-done | bytes 786464 | tf_op jit(solution)/shard_map/ppermute | solution.py:17
  123.5 76.1 %all_gather.42 = s32[2,2048]{1,0:T(2,128)S(1)} all-gather(s32[2,512]{1,0:T(2,128)S(1)} %copy-done.37), channel_id=1, replica_groups=mesh['dp'=4,'ctx'=4,'tp'=2] {'ctx'}, dimensions={1}, use_global_device_ids=true | all-gather | bytes 20480 | tf_op jit(solution)/shard_map/all_gather | solution.py:142
  199.6 11.3 all_gather.43
  215.7 73.6 %while.26 = (s32[]{:T(128)}, bf16[2,512,6,64]{1,3,2,0:T(8,128)(2,1)}, f32[2,6,512]{2,1,0:T(8,128)S(1)}, bf16[2,2048,6,64]{1,3,2,0:T(8,128)(2,1)}, s32[2,512]{1,0...) while((s32[]{:T(128)}, ...), condition=%wide.region_3.4_spmd, body=%wide.region_0.3_spmd.sunk | while | flops 1687352320 | bytes 96358544 | solution.py:157
  216.4 11.7 %fusion.139 = (f32[6,512]{1,0:T(8,128)S(1)}, f32[6,512,2048]{2,1,0:T(8,128)}) fusion(pred[512,2048]{1,0:T(8,128)(4,1)S(1)} %broadcast_compare_fusion.4, bf16[2,2048,6,64]{1,3,2,0:T(8,128)(2,1)S(1)} %get-tuple-element.432, s32[]{:T(128)S(6)} %copy.81, bf16[2,512,6,64]{1,3,2,0:T(8,128)(2,1)} %get-tuple-element.431), kind=kOutput, calls=%fused_computation.3.clone.1 | convolution fusion | flops 824177664 | bytes 28193792 | tf_op jit(solution)/shard_map/while/body/eval_jaxpr/qhd,khd->hqk/dot_general | solution.py:81
  228.0 12.1 %fusion.140 = f32[6,512]{1,0:T(8,128)S(1)} fusion(f32[6,512,2048]{2,1,0:T(8,128)} %get-tuple-element.390, f32[6,512]{1,0:T(8,128)S(1)} %get-tuple-element.391, pred[512,2048]{1,0:T(8,128)(4,1)S(1)} %broadcast_compare_fusion.4), kind=kLoop, calls=%fused_computation.4.clone.1 | loop fusion | flops 25162752 | bytes 26238976 | tf_op jit(solution)/shard_map/while/body/eval_jaxpr/reduce_sum | solution.py:152
  240.2 12.3 %fusion.141 = bf16[2,512,6,64]{1,3,2,0:T(8,128)(2,1)} fusion(bf16[2,512,6,64]{1,3,2,0:T(8,128)(2,1)} %get-tuple-element.417, s32[]{:T(128)S(6)} %copy.81, f32[6,512,2048]{2,1,0:T(8,128)} %get-tuple-element.390, f32[6,512]{1,0:T(8,128)S(1)} %fusion.140, f32[6,512]{1,0:T(8,128)S(1)} %get-tuple-element.391, ...), kind=kOutput, calls=%fused_computation.14.clone.1 | convolution fusion | flops 836960256 | bytes 28214272 | tf_op jit(solution)/shard_map/while/body/eval_jaxpr/hqk,khd->qhd/dot_general | solution.py:154
  253.2 11.7 %fusion.139 = (f32[6,512]{1,0:T(8,128)S(1)}, f32[6,512,2048]{2,1,0:T(8,128)}) fusion(pred[512,2048]{1,0:T(8,128)(4,1)S(1)} %broadcast_compare_fusion.4, bf16[2,2048,6,64]{1,3,2,0:T(8,128)(2,1)S(1)} %get-tuple-element.432, s32[]{:T(128)S(6)} %copy.81, bf16[2,512,6,64]{1,3,2,0:T(8,128)(2,1)} %get-tuple-element.431), kind=kOutput, calls=%fused_computation.3.clone.1 | convolution fusion | flops 824177664 | bytes 28193792 | tf_op jit(solution)/shard_map/while/body/eval_jaxpr/qhd,khd->hqk/dot_general | solution.py:81
  264.9 12.1 %fusion.140 = f32[6,512]{1,0:T(8,128)S(1)} fusion(f32[6,512,2048]{2,1,0:T(8,128)} %get-tuple-element.390, f32[6,512]{1,0:T(8,128)S(1)} %get-tuple-element.391, pred[512,2048]{1,0:T(8,128)(4,1)S(1)} %broadcast_compare_fusion.4), kind=kLoop, calls=%fused_computation.4.clone.1 | loop fusion | flops 25162752 | bytes 26238976 | tf_op jit(solution)/shard_map/while/body/eval_jaxpr/reduce_sum | solution.py:152
  277.0 12.3 %fusion.141 = bf16[2,512,6,64]{1,3,2,0:T(8,128)(2,1)} fusion(bf16[2,512,6,64]{1,3,2,0:T(8,128)(2,1)} %get-tuple-element.417, s32[]{:T(128)S(6)} %copy.81, f32[6,512,2048]{2,1,0:T(8,128)} %get-tuple-element.390, f32[6,512]{1,0:T(8,128)S(1)} %fusion.140, f32[6,512]{1,0:T(8,128)S(1)} %get-tuple-element.391, ...), kind=kOutput, calls=%fused_computation.14.clone.1 | convolution fusion | flops 836960256 | bytes 28214272 | tf_op jit(solution)/shard_map/while/body/eval_jaxpr/hqk,khd->qhd/dot_general | solution.py:154
  298.3 9.3 all-reduce.11
  317.9 34.6 %all-gather.10.cloned.1.call-done = bf16[768,1536]{1,0:T(8,128)(2,1)} async-done(((bf16[192,1536]{1,0:T(8,128)(2,1)}), bf16[768,1536]{1,0:T(8,128)(2,1)}) %all-gather.10.cloned.1.call-update) | async-done | bytes 2359312 | tf_op jit(solution)/shard_map/all_gather | solution.py:106
  352.6 7.4 fusion.96
  360.0 31.6 %all-gather.12.cloned.1.call-done = bf16[768,1536]{1,0:T(8,128)(2,1)} async-done(((bf16[192,1536]{1,0:T(8,128)(2,1)}), bf16[768,1536]{1,0:T(8,128)(2,1)}) %all-gather.12.cloned.1.call-update) | async-done | bytes 2359312 | tf_op jit(solution)/shard_map/all_gather | solution.py:107
  391.6 10.6 multiply_convert_fusion.3
  402.2 28.5 %all-gather.14.cloned.1.call-done = bf16[768,1536]{1,0:T(8,128)(2,1)} async-done(((bf16[192,1536]{1,0:T(8,128)(2,1)}), bf16[768,1536]{1,0:T(8,128)(2,1)}) %all-gather.14.cloned.1.call-update) | async-done | bytes 2359312 | tf_op jit(solution)/shard_map/all_gather | solution.py:108
  430.7 6.4 convolution_convert_fusion.5
  439.4 18.2 %all-reduce.20.cloned.1.call-done = bf16[1024,768]{1,0:T(8,128)(2,1)} async-done(((bf16[1024,768]{1,0:T(8,128)(2,1)}), bf16[1024,768]{1,0:T(8,128)(2,1)}) %all-reduce.20.cloned.1.call-update) | async-done | bytes 1572880 | tf_op jit(solution)/shard_map/psum | solution.py:171
  467.3 6.8 multiply_convert_fusion.1
  481.4 21.6 %all-reduce.22.cloned.1.call-done = bf16[1024,768]{1,0:T(8,128)(2,1)} async-done(((bf16[1024,768]{1,0:T(8,128)(2,1)}), bf16[1024,768]{1,0:T(8,128)(2,1)}) %all-reduce.22.cloned.1.call-update) | async-done | bytes 1572880 | tf_op jit(solution)/shard_map/psum | solution.py:208
  503.1 5.0 multiply_reduce_fusion.1
  521.5 161.5 %while.27 = (s32[]{:T(128)}, f32[2,512,6,64]{1,3,2,0:T(8,128)}, bf16[2,2048,384]{1,2,0:T(8,128)(2,1)}, bf16[2,2048,384]{1,2,0:T(8,128)(2,1)}, bf16[2,2048,6,64]{...) while((s32[]{:T(128)}, f32[2,512,6,64]{1,3,2,0:T(8,128)}, ...), condition=%wide.region_17.18_spmd, body=%wide.region_15.17_spmd.sunk | while | flops 4123718656 | bytes 245232944 | solution.py:240
  524.0 13.7 %fusion.150 = f32[6,512,2048]{2,1,0:T(8,128)} fusion(bf16[2,2048,6,64]{1,3,2,0:T(8,128)(2,1)} %copy-done.1, s32[]{:T(128)S(6)} %copy.95, bf16[2,512,6,64]{1,3,2,0:T(8,128)(2,1)} %get-tuple-element.465), kind=kOutput, calls=%fused_computation.36.clone.1 | convolution fusion | flops 805306368 | bytes 27132928 | tf_op jit(solution)/shard_map/while/body/eval_jaxpr/qhd,khd->hqk/dot_general | solution.py:81
  537.7 12.8 %fusion.152 = bf16[6,64,2048]{2,1,0:T(8,128)(2,1)} fusion(f32[6,512,2048]{2,1,0:T(8,128)} %fusion.150, f32[6,512]{1,0:T(8,128)S(1)} %dynamic-slice_bitcast_fusion.2, pred[512,2048]{1,0:T(8,128)(4,1)S(1)} %broadcast_compare_fusion.5, bf16[2,512,6,64]{1,3,2,0:T(8,128)(2,1)S(1)} %copy-done.19, s32[]{:T(128)S(6)} %copy.95), kind=kOutput, calls=%fused_computation.28.clone.1 | convolution fusion | flops 830472192 | bytes 28196868 | tf_op jit(solution)/shard_map/while/body/eval_jaxpr/hqk,qhd->khd/dot_general | solution.py:232
  550.5 20.0 %multiply_reduce_fusion.7 = (f32[6,512]{1,0:T(8,128)S(1)}, f32[6,512,2048]{2,1,0:T(8,128)}) fusion(f32[6,512,2048]{2,1,0:T(8,128)} %fusion.150, f32[6,512]{1,0:T(8,128)S(1)} %dynamic-slice_bitcast_fusion.2, pred[512,2048]{1,0:T(8,128)(4,1)S(1)} %broadcast_compare_fusion.5, bf16[2,2048,6,64]{1,3,2,0:T(8,128)(2,1)} %get-tuple-element.468, ...), kind=kOutput, calls=%fused_computation.25.clone.1 | convolution fusion | flops 836760576 | bytes 53376000 | tf_op jit(solution)/shard_map/while/body/eval_jaxpr/qhd,khd->hqk/dot_general | solution.py:219
  570.5 17.8 %multiply_convert_fusion.5 = bf16[6,512,2048]{2,1,0:T(8,128)(2,1)S(1)} fusion(f32[6,512,2048]{2,1,0:T(8,128)} %get-tuple-element.403, f32[6,512,2048]{2,1,0:T(8,128)} %fusion.150, f32[6,512]{1,0:T(8,128)S(1)} %get-tuple-element.404, f32[6,512]{1,0:T(8,128)S(1)} %dynamic-slice_bitcast_fusion.2, pred[512,2048]{1,0:T(8,128)(4,1)} %copy-done), kind=kLoop, calls=%fused_computation.24.clone.1 | loop fusion | flops 37748736 | bytes 63987712 | tf_op jit(solution)/shard_map/while/body/eval_jaxpr/convert_element_type | solution.py:223
  591.8 6.2 fusion.151
  604.5 13.7 %fusion.150 = f32[6,512,2048]{2,1,0:T(8,128)} fusion(bf16[2,2048,6,64]{1,3,2,0:T(8,128)(2,1)} %copy-done.1, s32[]{:T(128)S(6)} %copy.95, bf16[2,512,6,64]{1,3,2,0:T(8,128)(2,1)} %get-tuple-element.465), kind=kOutput, calls=%fused_computation.36.clone.1 | convolution fusion | flops 805306368 | bytes 27132928 | tf_op jit(solution)/shard_map/while/body/eval_jaxpr/qhd,khd->hqk/dot_general | solution.py:81
  618.2 12.8 %fusion.152 = bf16[6,64,2048]{2,1,0:T(8,128)(2,1)} fusion(f32[6,512,2048]{2,1,0:T(8,128)} %fusion.150, f32[6,512]{1,0:T(8,128)S(1)} %dynamic-slice_bitcast_fusion.2, pred[512,2048]{1,0:T(8,128)(4,1)S(1)} %broadcast_compare_fusion.5, bf16[2,512,6,64]{1,3,2,0:T(8,128)(2,1)S(1)} %copy-done.19, s32[]{:T(128)S(6)} %copy.95), kind=kOutput, calls=%fused_computation.28.clone.1 | convolution fusion | flops 830472192 | bytes 28196868 | tf_op jit(solution)/shard_map/while/body/eval_jaxpr/hqk,qhd->khd/dot_general | solution.py:232
  631.0 20.0 %multiply_reduce_fusion.7 = (f32[6,512]{1,0:T(8,128)S(1)}, f32[6,512,2048]{2,1,0:T(8,128)}) fusion(f32[6,512,2048]{2,1,0:T(8,128)} %fusion.150, f32[6,512]{1,0:T(8,128)S(1)} %dynamic-slice_bitcast_fusion.2, pred[512,2048]{1,0:T(8,128)(4,1)S(1)} %broadcast_compare_fusion.5, bf16[2,2048,6,64]{1,3,2,0:T(8,128)(2,1)} %get-tuple-element.468, ...), kind=kOutput, calls=%fused_computation.25.clone.1 | convolution fusion | flops 836760576 | bytes 53376000 | tf_op jit(solution)/shard_map/while/body/eval_jaxpr/qhd,khd->hqk/dot_general | solution.py:219
  651.0 17.8 %multiply_convert_fusion.5 = bf16[6,512,2048]{2,1,0:T(8,128)(2,1)S(1)} fusion(f32[6,512,2048]{2,1,0:T(8,128)} %get-tuple-element.403, f32[6,512,2048]{2,1,0:T(8,128)} %fusion.150, f32[6,512]{1,0:T(8,128)S(1)} %get-tuple-element.404, f32[6,512]{1,0:T(8,128)S(1)} %dynamic-slice_bitcast_fusion.2, pred[512,2048]{1,0:T(8,128)(4,1)} %copy-done), kind=kLoop, calls=%fused_computation.24.clone.1 | loop fusion | flops 37748736 | bytes 63987712 | tf_op jit(solution)/shard_map/while/body/eval_jaxpr/convert_element_type | solution.py:223
  672.2 6.3 fusion.151
  687.3 57.4 %reduce-scatter.10.cloned.1.call-done = bf16[2,512,384]{1,2,0:T(8,128)(2,1)} async-done(((bf16[2,2048,384]{1,2,0:T(8,128)(2,1)}), bf16[2,512,384]{1,2,0:T(8,128)(2,1)}) %reduce-scatter.10.cloned.1.call-update) | async-done | bytes 786448 | tf_op jit(solution)/shard_map/reduce_scatter | solution.py:244
  759.2 48.1 %reduce-scatter.12.cloned.1.call-done = bf16[2,512,384]{1,2,0:T(8,128)(2,1)} async-done(((bf16[2,2048,384]{1,2,0:T(8,128)(2,1)}), bf16[2,512,384]{1,2,0:T(8,128)(2,1)}) %reduce-scatter.12.cloned.1.call-update) | async-done | bytes 786448 | tf_op jit(solution)/shard_map/reduce_scatter | solution.py:247
  809.7 4.7 convolution_convert_fusion.3
  821.7 7.0 convolution_convert_fusion
  828.8 5.9 convolution_convert_fusion.2
  834.8 5.9 convolution_convert_fusion.1
  840.8 5.0 bitcast_convert_fusion
  845.9 5.0 reduce-scatter.22.cloned.1.call-done
  853.0 26.7 %reduce-scatter.14.cloned.1.call-done = bf16[192,384]{1,0:T(8,128)(2,1)} async-done(((bf16[768,384]{1,0:T(8,128)(2,1)}), bf16[192,384]{1,0:T(8,128)(2,1)}) %reduce-scatter.14.cloned.1.call-update) | async-done | bytes 147472 | tf_op jit(solution)/shard_map/reduce_scatter | solution.py:269
  879.7 40.5 %reduce-scatter.20.cloned.1.call-done = bf16[192,1536]{1,0:T(8,128)(2,1)} async-done(((bf16[768,1536]{1,0:T(8,128)(2,1)}), bf16[192,1536]{1,0:T(8,128)(2,1)}) %reduce-scatter.20.cloned.1.call-update) | async-done | bytes 589840 | tf_op jit(solution)/shard_map/reduce_scatter | solution.py:278
  920.1 40.3 %reduce-scatter.16.cloned.1.call-done = bf16[192,1536]{1,0:T(8,128)(2,1)} async-done(((bf16[768,1536]{1,0:T(8,128)(2,1)}), bf16[192,1536]{1,0:T(8,128)(2,1)}) %reduce-scatter.16.cloned.1.call-update) | async-done | bytes 589840 | tf_op jit(solution)/shard_map/reduce_scatter | solution.py:272
  960.4 40.3 %reduce-scatter.18.cloned.1.call-done = bf16[192,1536]{1,0:T(8,128)(2,1)} async-done(((bf16[768,1536]{1,0:T(8,128)(2,1)}), bf16[192,1536]{1,0:T(8,128)(2,1)}) %reduce-scatter.18.cloned.1.call-update) | async-done | bytes 589840 | tf_op jit(solution)/shard_map/reduce_scatter | solution.py:275
  1003.4 15.1 %all-reduce.10 = (bf16[768]{0:T(1024)(128)(2,1)S(1)}, bf16[768]{0:T(1024)(128)(2,1)S(1)}, bf16[768]{0:T(1024)(128)(2,1)S(1)}, bf16[768]{0:T(1024)(128)(2,1)S(1)}, bf16[768]{0:T(1024)(128)(2,1)S(1)}) all-reduce(bf16[768]{0:T(1024)(128)(2,1)S(1)} %dynamic-update-slice.3, ...), channel_id=1, replica_groups=mesh['dp'=4,'ctx'=4,'tp'=2] {'dp'}, use_global_device_ids=true, to_apply=%add.3 | all-reduce | flops 3840 | bytes 15360
  1018.7 11.7 %all-reduce.8 = (bf16[192]{0:T(256)(128)(2,1)S(1)}, bf16[192]{0:T(256)(128)(2,1)S(1)}, bf16[192]{0:T(256)(128)(2,1)S(1)}, bf16[192]{0:T(256)(128)(2,1)S(1)}) all-reduce(bf16[192]{0:T(256)(128)(2,1)S(1)} %dynamic-slice.5, bf16[192]{0:T(256)(128)(2,1)S(1)} %dynamic-slice.7, ...), channel_id=1, replica_groups=mesh['dp'=4,'ctx'=4,'tp'=2] {'ctx'}, use_global_device_ids=true, to_apply=%region_33.34 | all-reduce | flops 768 | bytes 3072 | tf_op jit(solution)/shard_map/psum | solution.py:300
  1038.2 90.7 %all-reduce.26.cloned.1.call-done = (bf16[192,3,384]{0,2,1:T(8,128)(2,1)}, bf16[192,384]{1,0:T(8,128)(2,1)}, bf16[192,1536]{1,0:T(8,128)(2,1)}, bf16[192,1536]{1,0:T(8,128)(2,1)}, bf16[192,1536]{1,0:T(8,128)(2,1)}) async-done(((bf16[192,3,384]{0,2,1:T(8,128)(2,1)}, bf16[192,384]{1,0:T(8,128)(2,1)}, bf16[192,1536]{1,0:T(8,128)(2,1)}, bf16[192,1536]{1,0:T(8,128)(2,1)}, bf16[192,1536]{1,0:T(8,128)(2,1)}), ...) | async-done | bytes 2359312 | tf_op jit(solution)/shard_map/psum | solution.py:295
  (296 shorter events, 146.1 us)
Async XLA Ops:
  7.2 40.5 %copy-start.6 = (bf16[2,512,768]{2,1,0:T(8,128)(2,1)S(1)}, bf16[2,512,768]{2,1,0:T(8,128)(2,1)}, u32[]{:S(2)}) copy-start(bf16[2,512,768]{2,1,0:T(8,128)(2,1)} %param.16) | copy-start | bytes 4718596
  7.2 37.9 %all-gather.6.cloned.1.call-start = ((), (), s32[]{:S(2)}) async-start(), calls=%async_computation.7 | async-start | bytes 2211840 | tf_op jit(solution)/shard_map/all_gather | solution.py:104
  7.9 207.7 %all-gather.8.cloned.1.call-start = ((), (), s32[]{:S(2)}) async-start(), calls=%async_computation.8 | async-start | bytes 3932160 | tf_op jit(solution)/shard_map/all_gather | solution.py:140
  52.9 259.4 %all-reduce.18.cloned.1.call-start = ((), (), s32[]{:S(2)}) async-start(), calls=%async_computation.9 | async-start | bytes 3145728 | tf_op jit(solution)/shard_map/psum | solution.py:159
  58.5 65.0 %copy-start.37 = (s32[2,512]{1,0:T(2,128)S(1)}, s32[2,512]{1,0:T(2,128)}, u32[]{:S(2)}) copy-start(s32[2,512]{1,0:T(2,128)} %param.17) | copy-start | bytes 12292
  58.5 141.1 %copy-start.38 = (bf16[192,384]{1,0:T(8,128)(2,1)S(1)}, bf16[192,384]{1,0:T(8,128)(2,1)}, u32[]{:S(2)}) copy-start(bf16[192,384]{1,0:T(8,128)(2,1)} %param.20) | copy-start | bytes 442372
  59.2 60.3 %collective-permute-start = (bf16[2,512,384]{1,2,0:T(8,128)(2,1)S(1)}, bf16[2,512,384]{1,2,0:T(8,128)(2,1)S(1)}, u32[]{:S(2)}, u32[]{:S(2)}) collective-permute-start(bf16[2,512,384]{1,2,0:T(8,128)(2,1)S(1)} %fusion.80), channel_id=1, source_target_pairs={{0,2},{2,0},{4,6},{6,4},{1,3},{3,1},{5,7},{7,5},{8,10},{10,8},{12,... | collective-permute-start | bytes 2359304 | tf_op jit(solution)/shard_map/ppermute | solution.py:17
  121.1 90.3 %collective-permute-start.1 = (bf16[2,1024,384]{1,2,0:T(8,128)(2,1)}, bf16[2,1024,384]{1,2,0:T(8,128)(2,1)S(1)}, u32[]{:S(2)}, u32[]{:S(2)}) collective-permute-start(bf16[2,1024,384]{1,2,0:T(8,128)(2,1)} %maximum_select_fusion.2), channel_id=1, source_target_pairs={{0,4},{2,6},{4,0},{6,2},{1,5},{3,7},{5,1},{7,3},{8,12},{10,14},{12... | collective-permute-start | bytes 4718600 | tf_op jit(solution)/shard_map/ppermute | solution.py:17
  228.0 12.1 %copy-start.17 = (bf16[2,2048,6,64]{1,3,2,0:T(8,128)(2,1)S(1)}, bf16[2,2048,6,64]{1,3,2,0:T(8,128)(2,1)}, u32[]{:S(2)}) copy-start(bf16[2,2048,6,64]{1,3,2,0:T(8,128)(2,1)} %get-tuple-element.428) | copy-start | bytes 9437188 | tf_op jit(solution)/shard_map/while
  264.9 12.1 %copy-start.17 = (bf16[2,2048,6,64]{1,3,2,0:T(8,128)(2,1)S(1)}, bf16[2,2048,6,64]{1,3,2,0:T(8,128)(2,1)}, u32[]{:S(2)}) copy-start(bf16[2,2048,6,64]{1,3,2,0:T(8,128)(2,1)} %get-tuple-element.428) | copy-start | bytes 9437188 | tf_op jit(solution)/shard_map/while
  294.6 58.0 %all-gather.10.cloned.1.call-start = ((), (), s32[]{:S(2)}) async-start(), calls=%async_computation.10 | async-start | bytes 2949120 | tf_op jit(solution)/shard_map/all_gather | solution.py:106
  295.1 96.5 %all-gather.12.cloned.1.call-start = ((), (), s32[]{:S(2)}) async-start(), calls=%async_computation.11 | async-start | bytes 2949120 | tf_op jit(solution)/shard_map/all_gather | solution.py:107
  295.7 135.0 %all-gather.14.cloned.1.call-start = ((), (), s32[]{:S(2)}) async-start(), calls=%async_computation.12 | async-start | bytes 2949120 | tf_op jit(solution)/shard_map/all_gather | solution.py:108
  296.3 161.3 %all-reduce.20.cloned.1.call-start = ((), (), s32[]{:S(2)}) async-start(), calls=%async_computation.13 | async-start | bytes 3145728 | tf_op jit(solution)/shard_map/psum | solution.py:171
  437.1 65.9 %all-reduce.22.cloned.1.call-start = ((), (), s32[]{:S(2)}) async-start(), calls=%async_computation.14 | async-start | bytes 3145728 | tf_op jit(solution)/shard_map/psum | solution.py:208
  437.6 27.9 %copy-start.39 = (f32[768]{0:T(1024)}, f32[768]{0:T(1024)S(1)}, u32[]{:S(2)}) copy-start(f32[768]{0:T(1024)S(1)} %convert_element_type.220) | copy-start | bytes 9220
  466.8 7.4 copy-start.14
  467.3 6.9 copy-start.49
  481.3 263.4 %reduce-scatter.10.cloned.1.call-start = ((), (), s32[]{:S(2)}) async-start(), calls=%async_computation.15 | async-start | bytes 3932160 | tf_op jit(solution)/shard_map/reduce_scatter | solution.py:244
  524.0 26.5 %copy-start = (pred[512,2048]{1,0:T(8,128)(4,1)}, pred[512,2048]{1,0:T(8,128)(4,1)S(1)}, u32[]{:S(2)}) copy-start(pred[512,2048]{1,0:T(8,128)(4,1)S(1)} %broadcast_compare_fusion.5) | copy-start | bytes 3145732 | tf_op jit(solution)/shard_map/while
  524.0 13.7 %copy-start.19 = (bf16[2,512,6,64]{1,3,2,0:T(8,128)(2,1)S(1)}, bf16[2,512,6,64]{1,3,2,0:T(8,128)(2,1)}, u32[]{:S(2)}) copy-start(bf16[2,512,6,64]{1,3,2,0:T(8,128)(2,1)} %get-tuple-element.467) | copy-start | bytes 2359300 | tf_op jit(solution)/shard_map/while
  570.5 17.8 %copy-start.5 = (bf16[2,512,6,64]{1,3,2,0:T(8,128)(2,1)S(1)}, bf16[2,512,6,64]{1,3,2,0:T(8,128)(2,1)}, u32[]{:S(2)}) copy-start(bf16[2,512,6,64]{1,3,2,0:T(8,128)(2,1)} %get-tuple-element.465) | copy-start | bytes 2359300 | tf_op jit(solution)/shard_map/while
  604.5 26.5 %copy-start = (pred[512,2048]{1,0:T(8,128)(4,1)}, pred[512,2048]{1,0:T(8,128)(4,1)S(1)}, u32[]{:S(2)}) copy-start(pred[512,2048]{1,0:T(8,128)(4,1)S(1)} %broadcast_compare_fusion.5) | copy-start | bytes 3145732 | tf_op jit(solution)/shard_map/while
  604.5 13.7 %copy-start.19 = (bf16[2,512,6,64]{1,3,2,0:T(8,128)(2,1)S(1)}, bf16[2,512,6,64]{1,3,2,0:T(8,128)(2,1)}, u32[]{:S(2)}) copy-start(bf16[2,512,6,64]{1,3,2,0:T(8,128)(2,1)} %get-tuple-element.467) | copy-start | bytes 2359300 | tf_op jit(solution)/shard_map/while
  651.0 17.8 %copy-start.5 = (bf16[2,512,6,64]{1,3,2,0:T(8,128)(2,1)S(1)}, bf16[2,512,6,64]{1,3,2,0:T(8,128)(2,1)}, u32[]{:S(2)}) copy-start(bf16[2,512,6,64]{1,3,2,0:T(8,128)(2,1)} %get-tuple-element.465) | copy-start | bytes 2359300 | tf_op jit(solution)/shard_map/while
  683.0 124.3 %reduce-scatter.12.cloned.1.call-start = ((), (), s32[]{:S(2)}) async-start(), calls=%async_computation.16 | async-start | bytes 3932160 | tf_op jit(solution)/shard_map/reduce_scatter | solution.py:247
  683.6 167.3 %reduce-scatter.22.cloned.1.call-start = ((), (), s32[]{:S(2)}) async-start(), calls=%async_computation.22 | async-start | bytes 2211840
  685.7 60.4 %copy-start.22 = (f32[2,512,6,64]{1,3,2,0:T(8,128)S(1)}, f32[2,512,6,64]{1,3,2,0:T(8,128)}, u32[]{:S(2)}) copy-start(f32[2,512,6,64]{1,3,2,0:T(8,128)} %get-tuple-element.115) | copy-start | bytes 4718596
  685.7 60.4 %copy-start.30 = (f32[512,64]{0,1:T(8,128)S(1)}, f32[512,64]{0,1:T(8,128)}, u32[]{:S(2)}) copy-start(f32[512,64]{0,1:T(8,128)} %copy-done.29) | copy-start | bytes 393220
  756.1 53.6 %copy-start.9 = (bf16[2,512,768]{2,1,0:T(8,128)(2,1)S(1)}, bf16[2,512,768]{2,1,0:T(8,128)(2,1)}, u32[]{:S(2)}) copy-start(bf16[2,512,768]{2,1,0:T(8,128)(2,1)} %param.16) | copy-start | bytes 4718596
  818.4 61.3 %reduce-scatter.14.cloned.1.call-start = ((), (), s32[]{:S(2)}) async-start(), calls=%async_computation.18 | async-start | bytes 737280 | tf_op jit(solution)/shard_map/reduce_scatter | solution.py:269
  821.6 7.1 copy-start.32
  821.6 98.5 %reduce-scatter.20.cloned.1.call-start = ((), (), s32[]{:S(2)}) async-start(), calls=%async_computation.21 | async-start | bytes 2949120 | tf_op jit(solution)/shard_map/reduce_scatter | solution.py:278
  828.7 131.7 %reduce-scatter.16.cloned.1.call-start = ((), (), s32[]{:S(2)}) async-start(), calls=%async_computation.19 | async-start | bytes 2949120 | tf_op jit(solution)/shard_map/reduce_scatter | solution.py:272
  834.7 6.1 copy-start.31
  834.7 166.0 %reduce-scatter.18.cloned.1.call-start = ((), (), s32[]{:S(2)}) async-start(), calls=%async_computation.20 | async-start | bytes 2949120 | tf_op jit(solution)/shard_map/reduce_scatter | solution.py:275
  840.7 193.7 %all-reduce.24.cloned.1.call-start = ((), (), s32[]{:S(2)}) async-start(), calls=%async_computation.17 | async-start | bytes 3145728 | tf_op jit(solution)/shard_map/psum | solution.py:261
  845.8 157.3 %copy-start.55 = (bf16[192]{0:T(256)(128)(2,1)S(1)}, bf16[192]{0:T(256)(128)(2,1)}, u32[]{:S(2)}) copy-start(bf16[192]{0:T(256)(128)(2,1)} %param.27) | copy-start | bytes 1156
  845.8 157.6 %copy-start.45 = (bf16[768]{0:T(1024)(128)(2,1)S(1)}, bf16[768]{0:T(1024)(128)(2,1)}, u32[]{:S(2)}) copy-start(bf16[768]{0:T(1024)(128)(2,1)} %get-tuple-element.186) | copy-start | bytes 4612
  845.8 157.6 %copy-start.46 = (bf16[768]{0:T(1024)(128)(2,1)S(1)}, bf16[768]{0:T(1024)(128)(2,1)}, u32[]{:S(2)}) copy-start(bf16[768]{0:T(1024)(128)(2,1)} %get-tuple-element.184) | copy-start | bytes 4612
  845.8 157.6 %copy-start.47 = (bf16[768]{0:T(1024)(128)(2,1)S(1)}, bf16[768]{0:T(1024)(128)(2,1)}, u32[]{:S(2)}) copy-start(bf16[768]{0:T(1024)(128)(2,1)} %get-tuple-element.189) | copy-start | bytes 4612
  845.8 186.9 %copy-start.4 = (f32[1024,768]{1,0:T(8,128)S(1)}, f32[1024,768]{1,0:T(8,128)}, u32[]{:S(2)}) copy-start(f32[1024,768]{1,0:T(8,128)} %copy-done.3) | copy-start | bytes 9437188
  845.8 186.9 %copy-start.40 = (f32[768]{0:T(1024)S(1)}, f32[768]{0:T(1024)}, u32[]{:S(2)}) copy-start(f32[768]{0:T(1024)} %copy-done.39) | copy-start | bytes 9220
  845.8 186.9 %copy-start.42 = (f32[1024]{0:T(1024)S(1)}, f32[1024]{0:T(1024)}, u32[]{:S(2)}) copy-start(f32[1024]{0:T(1024)} %copy-done.41) | copy-start | bytes 12292
  845.8 186.9 %copy-start.44 = (f32[1024]{0:T(1024)S(1)}, f32[1024]{0:T(1024)}, u32[]{:S(2)}) copy-start(f32[1024]{0:T(1024)} %copy-done.43) | copy-start | bytes 12292
  845.9 283.1 %all-reduce.26.cloned.1.call-start = ((), (), s32[]{:S(2)}) async-start(), calls=%async_computation.23 | async-start | bytes 5013504 | tf_op jit(solution)/shard_map/psum | solution.py:295
  1128.9 6.2 copy-start.36
  1128.9 7.3 copy-start.35
  (39 other events, 129.9 us)
Sparse Core Ops, SparseCore 0:
  9.8 35.1 all-gather.5
  53.0 82.9 all-gather.7
  294.7 17.5 all-reduce.17
  314.0 38.5 all-gather.9
  354.2 37.3 all-gather.11
  393.3 37.3 all-gather.13
  437.2 20.3 all-reduce.19
  481.5 21.5 all-reduce.21
  683.2 61.5 reduce-scatter.9
  746.9 60.3 reduce-scatter.11
  818.5 32.3 reduce-scatter.21
  854.2 25.3 reduce-scatter.13
  882.7 37.3 reduce-scatter.19
  923.0 37.3 reduce-scatter.15
  963.3 37.3 reduce-scatter.17
  1003.5 20.3 all-reduce.23
  1027.1 101.7 all-reduce.25
